TPU v7x, 32 devices: a whole 2x2x4 slice. The times are simulated.
32 devices in a mesh: dp: 8 (over z, x), tensor: 4 (over y, core).
Axes of the slice: x: 2, y: 2, z: 4, core: 2. Of those that a mesh axis runs over, the one named last changes fastest.
Arguments:
- query_states: bfloat16 [1, 8192, 1024], P(None, 'dp', 'tensor'), may hold values from -6 to 6
- key_states: bfloat16 [1, 8192, 1024], P(None, 'dp', 'tensor'), may hold values from -6 to 6
- value_states: bfloat16 [1, 8192, 1024], P(None, 'dp', 'tensor'), may hold values from -6 to 6
- joining_weight: bfloat16 [1, 1024, 2048], P(None, 'tensor'), may hold values from -0.1875 to 0.1875
- norm_gain: float32 [2048], replicated, may hold values from 0.1 to 1.9
- next_hidden: bfloat16 [8192, 2048], P(('dp', 'tensor')), may hold values from -6 to 6
- lengths: int32 [8], P('dp'), may hold values from 256 to 1024
- vote_counts: int32 [8], P('dp'), may hold values from 1 to 8
Outputs:
- draft_hidden: bfloat16 [8192, 2048], P(('dp', 'tensor'))
- weight_grad: bfloat16 [1, 1024, 2048], P(None, 'tensor', 'dp')
- gain_grad: float32 [2048], replicated
- draft_loss: float32 [], replicated
All inputs are finite; a program needn't handle non-finite values.
Results may differ from a plain program's by a relative error of at most 0.014.
Values may be sent and summed in bfloat16 or wider, within the bound.
No kernel may reach another device: no remote copies, remote signals or barrier semaphores. Data moves between devices by JAX's collectives and lax.ppermute only.
A program may use at most 64 MiB of HBM per device.

v0:
```python
import math
import jax
import jax.numpy as jnp
from jax import lax
from jax.sharding import PartitionSpec as P

HD = 128
loss_scale = 65536.0
neg_large = -1e30


def on_device(
    query_states,
    key_states,
    value_states,
    joining_weight,
    norm_gain,
    next_hidden,
    lengths,
    vote_counts,
):
    n_layers, tok_group, col_width = query_states.shape
    chains = lengths.shape[0]
    seq_len = tok_group // chains
    heads_here = col_width // HD
    shaped = (n_layers, chains, seq_len, heads_here, HD)
    scores = jnp.einsum(
        "lcqhd,lckhd->lchqk",
        query_states.reshape(shaped),
        key_states.reshape(shaped),
        preferred_element_type=jnp.float32,
    ) / math.sqrt(HD)
    positions = jnp.arange(seq_len)
    causal = positions[None, :] <= positions[:, None]
    key_valid = positions[None, :] < lengths[:, None]
    visible = causal[None, None, None, :, :] & key_valid[None, :, None, None, :]
    scores = jnp.where(visible, scores, neg_large)
    row_peak = jnp.max(scores, axis=-1, keepdims=True)
    exponent = jnp.exp(scores - row_peak)
    attn_probs = (exponent / jnp.sum(exponent, axis=-1, keepdims=True)).astype(jnp.bfloat16)
    context = jnp.einsum(
        "lchqk,lckhd->lcqhd",
        attn_probs,
        value_states.reshape(shaped),
        preferred_element_type=jnp.float32,
    )
    context = context.astype(jnp.bfloat16).reshape(n_layers, tok_group, col_width)
    own_rows = next_hidden.shape[0]
    offset = lax.axis_index("tensor") * own_rows
    partial_sum = jnp.einsum(
        "ltc,lcd->td", context, joining_weight, preferred_element_type=jnp.float32
    )
    summed = lax.psum(partial_sum.astype(jnp.bfloat16), "tensor").astype(jnp.float32)
    joined_rows = lax.dynamic_slice_in_dim(summed, offset, own_rows, 0)
    token_pos = offset + jnp.arange(own_rows, dtype=jnp.int32)
    chain_of = token_pos // seq_len
    in_chain = token_pos % seq_len
    onehot = (chain_of[:, None] == jnp.arange(chains)[None, :]).astype(jnp.float32)
    tok_votes = jnp.dot(onehot, vote_counts.astype(jnp.float32), precision=lax.Precision.HIGHEST)
    tok_length = jnp.dot(onehot, lengths.astype(jnp.float32), precision=lax.Precision.HIGHEST)
    token_weight = jnp.where(in_chain.astype(jnp.float32) < tok_length - 1.0, tok_votes, 0.0)
    inv_rms = lax.rsqrt(jnp.mean(joined_rows * joined_rows, axis=-1, keepdims=True) + 1e-06)
    normed = joined_rows * inv_rms
    predicted = normed * norm_gain
    draft_hidden = predicted.astype(jnp.bfloat16)
    misfit = predicted - next_hidden.astype(jnp.float32)
    local_loss = jnp.sum(token_weight * jnp.mean(misfit * misfit, axis=-1))
    grad_pred = loss_scale * 2.0 / joined_rows.shape[1] * token_weight[:, None] * misfit
    local_gain = jnp.sum(grad_pred * normed, axis=0)
    grad_normed = grad_pred * norm_gain
    grad_joined = (
        inv_rms * (grad_normed - normed * jnp.mean(grad_normed * normed, axis=-1, keepdims=True))
    ).astype(jnp.bfloat16)
    gain_sum, loss_sum, weight_total = lax.psum(
        (local_gain, local_loss, jnp.sum(token_weight)), ("dp", "tensor")
    )
    grad_total = jnp.einsum(
        "ltc,td->lcd",
        context,
        lax.all_gather(grad_joined, "tensor", axis=0, tiled=True),
        preferred_element_type=jnp.float32,
    )
    grad_cols = lax.psum_scatter(
        grad_total.astype(jnp.bfloat16), "dp", scatter_dimension=2, tiled=True
    ).astype(jnp.float32)
    weight_grad = (grad_cols / weight_total).astype(jnp.bfloat16)
    return (draft_hidden, weight_grad, gain_sum / weight_total, loss_sum / weight_total)


def solution(mesh):
    return jax.shard_map(
        on_device,
        mesh=mesh,
        in_specs=(
            P(None, "dp", "tensor"),
            P(None, "dp", "tensor"),
            P(None, "dp", "tensor"),
            P(None, "tensor", None),
            P(),
            P(("dp", "tensor"), None),
            P("dp"),
            P("dp"),
        ),
        out_specs=(P(("dp", "tensor"), None), P(None, "tensor", "dp"), P(), P()),
        check_vma=False,
    )
```

profile of v0, /device:TPU:0, one launch (start us, length us, event | category | flops | bytes accessed | tf_op | source)
XLA Modules:
  0.0 236.3 jit_solution(4800602347688197091)
XLA Ops:
  7.2 0.0 copy-start
  7.2 0.0 copy-start.2
  7.2 0.0 copy-start.3
  7.2 0.0 all-reduce.3.cloned.1.call-start
  8.0 0.4 fusion.4
  8.4 2.0 reshape.122
  10.4 0.0 copy-done.2
  10.4 1.0 reshape.123
  11.4 0.0 copy-done.3
  11.4 1.0 copy.17
  12.4 0.0 copy-start.4
  12.4 7.7 %fusion.39 = (f32[2,1024]{1,0:T(2,128)S(1)}, f32[2,1024,1024]{1,2,0:T(8,128)}) fusion(pred[1024,1024]{0,1:T(8,128)(4,1)S(1)} %fusion.4, bf16[1024,2,128]{2,1,0:T(2,128)(2,1)} %reshape.123, bf16[1024,2,128]{2,1,0:T(2,128)(2,1)} %reshape.122), kind=kOutput, calls=%fused_computation.54 | convolution fusion | flops 545260544 | bytes 10493952 | tf_op jit(solution)/shard_map/sub | solution.py:39
  20.1 0.0 copy-done.4
  20.1 4.1 %fusion.20 = bf16[2,1024,128]{1,2,0:T(8,128)(2,1)S(1)} fusion(bf16[1024,2,128]{0,2,1:T(8,128)(2,1)S(1)} %bitcast.23, f32[2,1024,1024]{1,2,0:T(8,128)} %get-tuple-element.13, f32[2,1024]{1,0:T(2,128)S(1)} %get-tuple-element.12), kind=kOutput, calls=%fused_computation.29 | convolution fusion | flops 541327360 | bytes 9445376 | tf_op jit(solution)/shard_map/lchqk,lckhd->lcqhd/dot_general | solution.py:41
  24.3 0.0 copy-done
  24.3 3.3 %convolution_convert_fusion = bf16[1024,2048]{1,0:T(8,128)(2,1)} fusion(bf16[1024,256]{0,1:T(8,128)(2,1)S(1)} %bitcast.21, bf16[1,256,2048]{2,1,0:T(8,128)(2,1)S(1)} %copy-done), kind=kOutput, calls=%fused_computation.11 | convolution fusion | flops 1075838976 | bytes 5767168 | tf_op jit(solution)/shard_map/ltc,lcd->td/dot_general | solution.py:50
  27.5 0.0 copy-start.1
  27.5 0.0 copy-start.5
  27.5 0.0 all-reduce.3.cloned.1.call-update
  27.6 0.0 all-gather.2.cloned.1.call-start
  28.3 0.6 broadcast_multiply_fusion
  29.0 86.9 %all-reduce.3.cloned.1.call-done = bf16[1024,2048]{1,0:T(8,128)(2,1)} async-done(((bf16[1024,2048]{1,0:T(8,128)(2,1)}), bf16[1024,2048]{1,0:T(8,128)(2,1)}) %all-reduce.3.cloned.1.call-update) | async-done | bytes 4194320 | tf_op jit(solution)/shard_map/psum | solution.py:53
  115.9 1.5 fusion.19
  117.4 0.0 copy-done.1
  117.4 0.0 copy-done.5
  117.4 2.3 fusion.18
  119.8 3.4 %fusion.17 = (bf16[256,2048]{1,0:T(8,128)(2,1)}, bf16[256,2048]{1,0:T(8,128)(2,1)}) fusion(bf16[256,2048]{1,0:T(8,128)(2,1)S(1)} %copy-done.1, f32[256]{0:T(256)S(1)} %broadcast_multiply_fusion.1, f32[256]{0:T(256)S(1)} %get-tuple-element.14, f32[2048]{0:T(1024)S(1)} %copy-done.5, f32[256]{0:T(256)S(1)} %add_rsqrt_fusion, ...), kind=kLoop, calls=%fused_computation.25 | loop fusion | flops 6291456 | bytes 4205572 | tf_op jit(solution)/shard_map/convert_element_type | solution.py:73
  123.2 0.0 all-gather.2.cloned.1.call-update
  123.2 0.0 reduce-scatter.2.cloned.1.call-start
  123.3 34.7 %all-gather.2.cloned.1.call-done = bf16[1024,2048]{1,0:T(8,128)(2,1)} async-done(((bf16[256,2048]{1,0:T(8,128)(2,1)}), bf16[1024,2048]{1,0:T(8,128)(2,1)}) %all-gather.2.cloned.1.call-update) | async-done | bytes 4194320 | tf_op jit(solution)/shard_map/all_gather | solution.py:80
  158.0 4.4 %fusion.11 = bf16[1,256,2048]{2,1,0:T(8,128)(2,1)} fusion(bf16[1024,256]{0,1:T(8,128)(2,1)S(1)} %bitcast.22, bf16[1024,2048]{1,0:T(8,128)(2,1)} %all-gather.2.cloned.1.call-done), kind=kOutput, calls=%fused_computation.19 | convolution fusion | flops 1074266112 | bytes 5767168 | tf_op jit(solution)/shard_map/ltc,td->lcd/dot_general | solution.py:77
  162.4 0.0 reduce-scatter.2.cloned.1.call-update
  162.4 0.7 multiply_reduce_fusion.1
  163.1 39.7 %all-reduce = (f32[]{:T(128)}, f32[2048]{0:T(1024)S(1)}, f32[]{:T(128)}) all-reduce(f32[]{:T(128)} %get-tuple-element.15, f32[2048]{0:T(1024)S(1)} %get-tuple-element.4, f32[]{:T(128)} %multiply_reduce_fusion.1), channel_id=1, replica_groups=mesh['dp'=8,'tensor'=4] {'dp','tensor'}, use_global_device_ids=true, to_apply=%region_7.8 | all-reduce | flops 2050 | bytes 16400 | tf_op jit(solution)/shard_map/psum | solution.py:74
  204.1 1.2 broadcast_divide_fusion
  205.2 21.3 %reduce-scatter.2.cloned.1.call-done = bf16[1,256,256]{2,1,0:T(8,128)(2,1)} async-done(((bf16[1,256,2048]{2,1,0:T(8,128)(2,1)}), bf16[1,256,256]{2,1,0:T(8,128)(2,1)}) %reduce-scatter.2.cloned.1.call-update) | async-done | bytes 131088 | tf_op jit(solution)/shard_map/reduce_scatter | solution.py:83
  226.5 2.1 divide_convert_fusion.4
  (3 shorter events, 0.0 us)
Async XLA Ops:
  7.2 17.1 %copy-start = (bf16[1,256,2048]{2,1,0:T(8,128)(2,1)S(1)}, bf16[1,256,2048]{2,1,0:T(8,128)(2,1)}, u32[]{:S(2)}) copy-start(bf16[1,256,2048]{2,1,0:T(8,128)(2,1)} %param.11) | copy-start | bytes 3145732
  7.2 3.3 %copy-start.2 = (bf16[1,1024,256]{2,1,0:T(8,128)(2,1)S(1)}, bf16[1,1024,256]{2,1,0:T(8,128)(2,1)}, u32[]{:S(2)}) copy-start(bf16[1,1024,256]{2,1,0:T(8,128)(2,1)} %param.9) | copy-start | bytes 1572868
  7.2 4.2 %copy-start.3 = (bf16[1,1024,256]{2,1,0:T(8,128)(2,1)S(1)}, bf16[1,1024,256]{2,1,0:T(8,128)(2,1)}, u32[]{:S(2)}) copy-start(bf16[1,1024,256]{2,1,0:T(8,128)(2,1)} %param.10) | copy-start | bytes 1572868
  7.2 108.7 %all-reduce.3.cloned.1.call-start = ((), (), s32[]{:S(2)}) async-start(), calls=%async_computation.1 | async-start | bytes 8388608 | tf_op jit(solution)/shard_map/psum | solution.py:53
  12.4 7.7 %copy-start.4 = (bf16[1,1024,256]{1,2,0:T(8,128)(2,1)S(1)}, bf16[1,1024,256]{1,2,0:T(8,128)(2,1)}, u32[]{:S(2)}) copy-start(bf16[1,1024,256]{1,2,0:T(8,128)(2,1)} %copy.17) | copy-start | bytes 1572868
  27.5 89.9 %copy-start.1 = (bf16[256,2048]{1,0:T(8,128)(2,1)S(1)}, bf16[256,2048]{1,0:T(8,128)(2,1)}, u32[]{:S(2)}) copy-start(bf16[256,2048]{1,0:T(8,128)(2,1)} %param.13) | copy-start | bytes 3145732
  27.5 89.9 %copy-start.5 = (f32[2048]{0:T(1024)S(1)}, f32[2048]{0:T(1024)}, u32[]{:S(2)}) copy-start(f32[2048]{0:T(1024)} %param.12) | copy-start | bytes 24580
  27.6 130.4 %all-gather.2.cloned.1.call-start = ((), (), s32[]{:S(2)}) async-start(), calls=%async_computation.2 | async-start | bytes 5242880 | tf_op jit(solution)/shard_map/all_gather | solution.py:80
  123.2 103.3 %reduce-scatter.2.cloned.1.call-start = ((), (), s32[]{:S(2)}) async-start(), calls=%async_computation.3 | async-start | bytes 1179648 | tf_op jit(solution)/shard_map/reduce_scatter | solution.py:83
Sparse Core Ops, SparseCore 0:
  27.7 88.1 all-reduce.2
  123.3 34.6 all-gather.1
  162.5 63.9 reduce-scatter.1
where the time goes:
time: 237 us; the launch traced here: 236 us
  waiting for transfers between devices  143 us (60%)
  blocking collectives  39.7 us (17%)
  matrix products  19.5 us (8%)
  between operations  17.7 us (7%)
  other arithmetic  12.2 us (5%)
  local copies, waits for them, and re-layouts  4.04 us (2%)
    psum x1, waiting for transfers between devices, on_device(): lax.psum(partial_sum.astype(jnp.bfloat16), 'tensor').astype(jnp.float32)  86.9 us
    psum x1, blocking collectives, on_device(): lax.psum((local_gain, local_loss, jnp.sum(token_weight)), ('dp', 'tensor'))  39.7 us
    all_gather x1, waiting for transfers between devices, on_device(): lax.all_gather(grad_joined, 'tensor', axis=0, tiled=True)  34.7 us
    reduce_scatter x1, waiting for transfers between devices, on_device(): lax.psum_scatter(grad_total.astype(jnp.bfloat16), 'dp', scatter_dimension...  21.3 us
    sub x1, matrix products, on_device(): exponent = jnp.exp(scores - row_peak)  7.73 us
  transfers between devices with their start and end apart: 3, of which 3 were waited for; matrix products, arithmetic and copies ran while one was open for 1% of the time, Pallas kernels for 0%

commit v1 on v0

--- a/solution.py
+++ b/solution.py
@@ -3,6 +3,7 @@
 import jax.numpy as jnp
 from jax import lax
 from jax.sharding import PartitionSpec as P
+from jax.lax import axis_index, axis_size, ppermute
 
 HD = 128
 loss_scale = 65536.0
@@ -74,11 +75,23 @@
     gain_sum, loss_sum, weight_total = lax.psum(
         (local_gain, local_loss, jnp.sum(token_weight)), ("dp", "tensor")
     )
+
+    def place_seats_all(at_axis, frame_in):
+        f_now, now = (axis_size("tensor"), axis_index("tensor"))
+        out_arr, z_new = (frame_in, 1)
+        while z_new < f_now:
+            arrivals = []
+            for h in tuple(range(f_now)):
+                arrivals.append((h, h ^ z_new))
+            carry_in = ppermute(out_arr, "tensor", perm=arrivals)
+            tmp = jnp.concatenate([out_arr, carry_in], axis=at_axis)
+            e_next = jnp.concatenate([carry_in, out_arr], axis=at_axis)
+            out_arr = jnp.where(now & z_new == 0, tmp, e_next)
+            z_new = 2 * z_new
+        return out_arr
+
     grad_total = jnp.einsum(
-        "ltc,td->lcd",
-        context,
-        lax.all_gather(grad_joined, "tensor", axis=0, tiled=True),
-        preferred_element_type=jnp.float32,
+        "ltc,td->lcd", context, place_seats_all(0, grad_joined), preferred_element_type=jnp.float32
     )
     grad_cols = lax.psum_scatter(
         grad_total.astype(jnp.bfloat16), "dp", scatter_dimension=2, tiled=True

time: 237 us -> 259 us (1.093)
  waiting for transfers between devices: 143 us -> 159 us
  other arithmetic: 12.2 us -> 15.7 us
    ppermute x0 -> x2, waiting for transfers between devices: none -> 50.3 us  [place_seats_all(): carry_in = ppermute(out_arr, 'tensor', perm=arrivals)]
    all_gather x1 -> x0, waiting for transfers between devices: 34.7 us -> none  [on_device(): lax.all_gather(grad_joined, 'tensor', axis=0, tiled=True)]
    select_n x0 -> x1, other arithmetic: none -> 3.82 us  [place_seats_all(): out_arr = jnp.where(now & z_new == 0, tmp, e_next)]
  transfers between devices with their start and end apart: 3 -> 4, of which waited for: 3 -> 4; matrix products, arithmetic and copies ran while one was open for 1% -> 1% of each run, Pallas kernels for 0% -> 0%
where the time goes in v1:
time: 259 us
  waiting for transfers between devices  159 us (61%)
  blocking collectives  39.9 us (15%)
  matrix products  20.7 us (8%)
  between operations  18 us (7%)
  other arithmetic  15.7 us (6%)
  local copies, waits for them, and re-layouts  5.23 us (2%)
    psum x1, waiting for transfers between devices, on_device(): lax.psum(partial_sum.astype(jnp.bfloat16), 'tensor').astype(jnp.float32)  87.5 us
    ppermute x2, waiting for transfers between devices, place_seats_all(): carry_in = ppermute(out_arr, 'tensor', perm=arrivals)  50.3 us
    psum x1, blocking collectives, on_device(): lax.psum((local_gain, local_loss, jnp.sum(token_weight)), ('dp', 'tensor'))  39.9 us
    reduce_scatter x1, waiting for transfers between devices, on_device(): lax.psum_scatter(grad_total.astype(jnp.bfloat16), 'dp', scatter_dimension...  20.7 us
    sub x1, matrix products, on_device(): exponent = jnp.exp(scores - row_peak)  7.53 us
    dot_general x1, matrix products, on_device(): jnp.einsum('ltc,td->lcd', context, place_seats_all(0, grad_joined), prefe...  5.74 us
  transfers between devices with their start and end apart: 4, of which 4 were waited for; matrix products, arithmetic and copies ran while one was open for 1% of the time, Pallas kernels for 0%

profile of v1, /device:TPU:0, one launch (start us, length us, event | category | flops | bytes accessed | tf_op | source)
XLA Modules:
  0.0 258.6 jit_solution(17393535471957651559)
XLA Ops:
  7.2 0.0 copy-start
  7.2 0.0 all-reduce.3.cloned.1.call-start
  8.0 0.4 fusion.10
  8.3 1.2 reshape.122
  9.5 2.0 reshape.123
  11.5 1.2 copy.17
  12.7 7.5 %fusion.48 = (f32[2,1024]{1,0:T(2,128)S(1)}, f32[2,1024,1024]{1,2,0:T(8,128)}) fusion(pred[1024,1024]{0,1:T(8,128)(4,1)S(1)} %fusion.10, bf16[1024,2,128]{2,1,0:T(2,128)(2,1)} %reshape.123, bf16[1024,2,128]{2,1,0:T(2,128)(2,1)S(1)} %reshape.122), kind=kOutput, calls=%fused_computation.64 | convolution fusion | flops 545260544 | bytes 10493952 | tf_op jit(solution)/shard_map/sub | solution.py:40
  20.2 4.1 %fusion.28 = bf16[2,1024,128]{1,2,0:T(8,128)(2,1)S(1)} fusion(bf16[1024,2,128]{0,2,1:T(8,128)(2,1)S(1)} %bitcast.22, f32[2,1024,1024]{1,2,0:T(8,128)} %get-tuple-element.13, f32[2,1024]{1,0:T(2,128)S(1)} %get-tuple-element.12), kind=kOutput, calls=%fused_computation.38 | convolution fusion | flops 541327360 | bytes 9445376 | tf_op jit(solution)/shard_map/lchqk,lckhd->lcqhd/dot_general | solution.py:42
  24.4 0.0 copy-start.2
  24.4 0.8 copy-done.2
  25.2 0.0 copy-done
  25.2 3.3 %convolution_convert_fusion = bf16[1024,2048]{1,0:T(8,128)(2,1)} fusion(bf16[1024,256]{0,1:T(8,128)(2,1)S(1)} %bitcast.20, bf16[1,256,2048]{2,1,0:T(8,128)(2,1)S(1)} %copy-done), kind=kOutput, calls=%fused_computation.19 | convolution fusion | flops 1075838976 | bytes 5767168 | tf_op jit(solution)/shard_map/ltc,lcd->td/dot_general | solution.py:51
  28.5 0.0 copy-start.1
  28.5 0.0 copy-start.4
  28.5 0.0 all-reduce.3.cloned.1.call-update
  28.5 0.0 reduce-scatter.2.cloned.1.call-start
  29.3 87.5 %all-reduce.3.cloned.1.call-done = bf16[1024,2048]{1,0:T(8,128)(2,1)} async-done(((bf16[1024,2048]{1,0:T(8,128)(2,1)}), bf16[1024,2048]{1,0:T(8,128)(2,1)}) %all-reduce.3.cloned.1.call-update) | async-done | bytes 4194320 | tf_op jit(solution)/shard_map/psum | solution.py:54
  116.9 1.5 fusion.27
  118.4 0.0 copy-done.1
  118.4 0.0 copy-done.4
  118.4 2.3 fusion.26
  120.8 3.0 %fusion.25 = (bf16[256,2048]{1,0:T(8,128)(2,1)S(1)}, bf16[256,2048]{1,0:T(8,128)(2,1)}) fusion(bf16[256,2048]{1,0:T(8,128)(2,1)S(1)} %copy-done.1, f32[256]{0:T(256)S(1)} %broadcast_multiply_fusion.1, f32[256]{0:T(256)S(1)} %broadcast_multiply_fusion, f32[2048]{0:T(1024)S(1)} %copy-done.4, f32[256]{0:T(256)S(1)} %add_rsqrt_fusion, ...), kind=kLoop, calls=%fused_computation.33 | loop fusion | flops 6291456 | bytes 4205572 | tf_op jit(solution)/shard_map/convert_element_type | solution.py:74
  123.8 0.0 copy-start.3
  123.8 0.0 collective-permute-start
  123.8 2.8 %collective-permute-done = bf16[256,2048]{1,0:T(8,128)(2,1)} collective-permute-done((bf16[256,2048]{1,0:T(8,128)(2,1)S(1)}, bf16[256,2048]{1,0:T(8,128)(2,1)}, u32[]{:S(2)}, u32[]{:S(2)}) %collective-permute-start) | collective-permute-done | bytes 1048608 | tf_op jit(solution)/shard_map/ppermute | solution.py:86
  126.6 3.8 %maximum_select_fusion.6 = bf16[512,2048]{1,0:T(8,128)(2,1)} fusion(bf16[256,2048]{1,0:T(8,128)(2,1)} %collective-permute-done, bf16[256,2048]{1,0:T(8,128)(2,1)S(1)} %get-tuple-element.10, pred[]{:T(512)S(6)} %eq.17), kind=kLoop, calls=%fused_computation.36 | loop fusion | flops 9437184 | bytes 4194305 | tf_op jit(solution)/shard_map/jit(_where)/select_n | solution.py:89
  130.4 0.5 collective-permute-start.1
  130.9 47.5 %collective-permute-done.1 = bf16[512,2048]{1,0:T(8,128)(2,1)} collective-permute-done((bf16[512,2048]{1,0:T(8,128)(2,1)}, bf16[512,2048]{1,0:T(8,128)(2,1)}, u32[]{:S(2)}, u32[]{:S(2)}) %collective-permute-start.1) | collective-permute-done | bytes 2097184 | tf_op jit(solution)/shard_map/ppermute | solution.py:86
  178.4 0.0 copy-done.3
  178.4 5.7 %fusion.19 = bf16[1,256,2048]{2,1,0:T(8,128)(2,1)} fusion(bf16[1024,256]{0,1:T(8,128)(2,1)S(1)} %bitcast.21, bf16[512,2048]{1,0:T(8,128)(2,1)} %collective-permute-done.1, bf16[512,2048]{1,0:T(8,128)(2,1)} %maximum_select_fusion.6, pred[]{:T(512)S(6)} %eq.16), kind=kOutput, calls=%fused_computation.27 | convolution fusion | flops 1093140480 | bytes 5767169 | tf_op jit(solution)/shard_map/ltc,td->lcd/dot_general | solution.py:93
  184.1 0.0 reduce-scatter.2.cloned.1.call-update
  184.2 0.6 fusion.44
  184.8 0.7 multiply_reduce_fusion.1
  185.4 39.9 %all-reduce = (f32[]{:T(128)}, f32[2048]{0:T(1024)S(1)}, f32[]{:T(128)}) all-reduce(f32[]{:T(128)} %fusion.44, f32[2048]{0:T(1024)S(1)} %get-tuple-element.4, f32[]{:T(128)} %multiply_reduce_fusion.1), channel_id=1, replica_groups=mesh['dp'=8,'tensor'=4] {'dp','tensor'}, use_global_device_ids=true, to_apply=%region_7.8 | all-reduce | flops 2050 | bytes 16400 | tf_op jit(solution)/shard_map/psum | solution.py:75
  226.6 1.2 broadcast_divide_fusion
  227.7 20.7 %reduce-scatter.2.cloned.1.call-done = bf16[1,256,256]{2,1,0:T(8,128)(2,1)} async-done(((bf16[1,256,2048]{2,1,0:T(8,128)(2,1)}), bf16[1,256,256]{2,1,0:T(8,128)(2,1)}) %reduce-scatter.2.cloned.1.call-update) | async-done | bytes 131088 | tf_op jit(solution)/shard_map/reduce_scatter | solution.py:96
  248.5 2.1 divide_convert_fusion.4
  (4 shorter events, 0.0 us)
Async XLA Ops:
  7.2 18.0 %copy-start = (bf16[1,256,2048]{2,1,0:T(8,128)(2,1)S(1)}, bf16[1,256,2048]{2,1,0:T(8,128)(2,1)}, u32[]{:S(2)}) copy-start(bf16[1,256,2048]{2,1,0:T(8,128)(2,1)} %param.11) | copy-start | bytes 3145732
  7.2 109.7 %all-reduce.3.cloned.1.call-start = ((), (), s32[]{:S(2)}) async-start(), calls=%async_computation.1 | async-start | bytes 8388608 | tf_op jit(solution)/shard_map/psum | solution.py:54
  24.4 0.8 copy-start.2
  28.5 89.9 %copy-start.1 = (bf16[256,2048]{1,0:T(8,128)(2,1)S(1)}, bf16[256,2048]{1,0:T(8,128)(2,1)}, u32[]{:S(2)}) copy-start(bf16[256,2048]{1,0:T(8,128)(2,1)} %param.13) | copy-start | bytes 3145732
  28.5 89.9 %copy-start.4 = (f32[2048]{0:T(1024)S(1)}, f32[2048]{0:T(1024)}, u32[]{:S(2)}) copy-start(f32[2048]{0:T(1024)} %param.12) | copy-start | bytes 24580
  28.5 220.0 %reduce-scatter.2.cloned.1.call-start = ((), (), s32[]{:S(2)}) async-start(), calls=%async_computation.2 | async-start | bytes 1179648 | tf_op jit(solution)/shard_map/reduce_scatter | solution.py:96
  123.8 54.6 %copy-start.3 = (bf16[2,1024,128]{1,2,0:T(8,128)(2,1)S(1)}, bf16[2,1024,128]{1,2,0:T(8,128)(2,1)}, u32[]{:S(2)}) copy-start(bf16[2,1024,128]{1,2,0:T(8,128)(2,1)} %copy-done.2) | copy-start | bytes 1572868
  123.8 2.8 %collective-permute-start = (bf16[256,2048]{1,0:T(8,128)(2,1)S(1)}, bf16[256,2048]{1,0:T(8,128)(2,1)}, u32[]{:S(2)}, u32[]{:S(2)}) collective-permute-start(bf16[256,2048]{1,0:T(8,128)(2,1)S(1)} %get-tuple-element.10), channel_id=1, source_target_pairs={{0,1},{1,0},{2,3},{3,2},{4,5},{5,4},{6,7},{7,6},{8,9},{9,8},{10,11... | collective-permute-start | bytes 3145736 | tf_op jit(solution)/shard_map/ppermute | solution.py:86
  130.4 48.0 %collective-permute-start.1 = (bf16[512,2048]{1,0:T(8,128)(2,1)}, bf16[512,2048]{1,0:T(8,128)(2,1)}, u32[]{:S(2)}, u32[]{:S(2)}) collective-permute-start(bf16[512,2048]{1,0:T(8,128)(2,1)} %maximum_select_fusion.6), channel_id=1, source_target_pairs={{0,2},{1,3},{2,0},{3,1},{4,6},{5,7},{6,4},{7,5},{8,10},{9,11},{10,... | collective-permute-start | bytes 6291464 | tf_op jit(solution)/shard_map/ppermute | solution.py:86
Sparse Core Ops, SparseCore 0:
  28.6 88.1 all-reduce.2
  184.3 64.1 reduce-scatter.1
